TPU v7x, 32 devices: a whole 2x2x4 slice. The times are simulated.
32 devices in a mesh: grp: 2 (over y), freq: 16 (over z, x, core).
Axes of the slice: x: 2, y: 2, z: 4, core: 2. Of those that a mesh axis runs over, the one named last changes fastest.
Arguments:
- source_field: bfloat16 [4, 16, 512, 256], P('grp', 'freq'), parts along dimension 0, may hold values from -6 to 6
- receiver_field: bfloat16 [4, 16, 512, 256], P('grp', 'freq'), parts along dimension 0, may hold values from -6 to 6
- slowness_slabs: bfloat16 [32, 768, 512], P(('grp', 'freq')), parts along dimension 0, may hold values from 0.3984375 to 1.1953125
- slab_map: int32 [4], P('grp'), parts along dimension 0, may hold values from 0 to 15
- reference_gaps: float32 [4, 3], P('grp'), parts along dimension 0, may hold values from 0.1 to 0.3
- reference_index: int32 [4, 512, 256], P('grp'), parts along dimension 0, may hold values from 0 to 1
- frequency_bins: int32 [16], replicated, may hold values from 10 to 120
- shot_corner: int32 [4], P('grp'), parts along dimension 0, may hold values from 0 to 256
Outputs:
- image: float32 [4, 512, 256, 256], P('grp', 'freq'), parts along dimension 0
There are 2 independent parts, one for each index of `grp`. A program takes and returns all parts, laid end to end along the dimension named above; an argument that names none is the same for every part. Nothing has to cross between parts.
All inputs are finite; a program needn't handle non-finite values.
Results may differ from a plain program's by a relative error of at most 0.014.
Values may be sent and summed in bfloat16 or wider, within the bound.
A program may use at most 128 MiB of HBM per device.

v0:
```python
import math
import jax
import jax.numpy as jnp
from jax import lax
from jax.sharding import PartitionSpec as P

LAGS = 256
DEPTHS = 2
cell_width = 0.0125
layer_thick = 0.0125
bin_hertz = 0.5
period_bins = 500
slow_base = 0.3


def spread(block, axis, holder):
    block = jnp.where(lax.axis_index(axis) == holder, block, jnp.zeros_like(block))
    return lax.psum(block, axis)


def transform_table(length, forward):
    grid_steps = jnp.arange(length, dtype=jnp.int32)
    phases = jnp.mod(grid_steps[:, None] * grid_steps[None, :], length).astype(jnp.float32)
    angles = phases * (2.0 * math.pi / length)
    norm_scale = 1.0 / math.sqrt(length)
    cosine = jnp.cos(angles) * norm_scale
    sine_part = jnp.sin(angles) * norm_scale
    if forward:
        cross_term = -sine_part
    else:
        cross_term = sine_part
    return jnp.stack([jnp.stack([cosine, cross_term]), jnp.stack([-cross_term, cosine])]).astype(
        jnp.bfloat16
    )


def wave_numbers(length):
    grid_steps = jnp.arange(length, dtype=jnp.int32)
    folded = jnp.where(grid_steps < length // 2, grid_steps, grid_steps - length).astype(
        jnp.float32
    )
    return folded * (2.0 * math.pi / (length * cell_width))


def lag_table(frequency_bins, lag_count):
    offsets = jnp.arange(lag_count, dtype=jnp.int32) - lag_count // 2
    cycles = jnp.mod(frequency_bins[:, None] * offsets[None, :], period_bins).astype(jnp.float32)
    angles = cycles * (2.0 * math.pi / period_bins)
    return jnp.stack([jnp.cos(angles), -jnp.sin(angles)]).astype(jnp.bfloat16)


def phase_factors(angular, references, squares):
    radicand = (angular * references[:, None, None]) ** 2 - squares[None]
    vertical = jnp.sqrt(jnp.maximum(radicand, 0.0))
    fading = jnp.exp(-jnp.sqrt(jnp.maximum(-radicand, 0.0)) * layer_thick)
    return (fading * jnp.cos(vertical * layer_thick), fading * jnp.sin(vertical * layer_thick))


def rotate(field_pair, turn_angle):
    return jnp.stack(
        [
            jnp.cos(turn_angle) * field_pair[:, 0] - jnp.sin(turn_angle) * field_pair[:, 1],
            jnp.cos(turn_angle) * field_pair[:, 1] + jnp.sin(turn_angle) * field_pair[:, 0],
        ],
        axis=1,
    )


def extrapolate(fields, angular, slowness, references, bracket, direction, tables, squares):
    forward_x, forward_y, inverse_x, inverse_y = tables
    half_done = jnp.einsum(
        "fcxy,cdyk->fdxk", fields, forward_y, preferred_element_type=jnp.float32
    ).astype(jnp.bfloat16)
    spectrum = jnp.einsum(
        "cdxk,fcxy->fdky", forward_x, half_done, preferred_element_type=jnp.float32
    )
    cos_part, sin_part = phase_factors(angular, references, squares)
    turned = direction[:, None, None, None] * sin_part[None]
    real_new = cos_part[None] * spectrum[:, None, 0] - turned * spectrum[:, None, 1]
    imag_new = cos_part[None] * spectrum[:, None, 1] + turned * spectrum[:, None, 0]
    shifted = jnp.stack([real_new, imag_new], axis=2).astype(jnp.bfloat16)
    returned = jnp.einsum(
        "cdxk,fjcxy->fjdky", inverse_x, shifted, preferred_element_type=jnp.float32
    ).astype(jnp.bfloat16)
    refocused = jnp.einsum(
        "fjcxy,cdyk->fjdxk", returned, inverse_y, preferred_element_type=jnp.float32
    )
    lower_pair = bracket == 0
    lower_field = jnp.where(lower_pair, refocused[:, 0], refocused[:, 1])
    upper_field = jnp.where(lower_pair, refocused[:, 1], refocused[:, 2])
    slow_low = jnp.where(lower_pair, references[0], references[1])
    slow_high = jnp.where(lower_pair, references[1], references[2])
    weight = jnp.clip((slowness - slow_low) / (slow_high - slow_low), 0.0, 1.0)
    turn_low = direction[:, None, None] * angular * layer_thick * (slowness - slow_low)[None]
    turn_high = direction[:, None, None] * angular * layer_thick * (slowness - slow_high)[None]
    mixed = (1.0 - weight) * rotate(lower_field, turn_low) + weight * rotate(upper_field, turn_high)
    return mixed.astype(jnp.bfloat16)


def lag_image_depths(cross_spec, lag_weights):
    total_bins = cross_spec.shape[2]
    summed = jnp.einsum(
        "dcwab,cwl->dabl", cross_spec, lag_weights, preferred_element_type=jnp.float32
    )
    return summed * total_bins ** (-0.5)


def cross_product(wave_stack):
    values = wave_stack.astype(jnp.float32)
    real_part = values[0, 0] * values[1, 0] + values[0, 1] * values[1, 1]
    imag_part = values[0, 0] * values[1, 1] - values[0, 1] * values[1, 0]
    return jnp.stack([real_part, imag_part]).astype(jnp.bfloat16)


def shards(
    source_field,
    receiver_field,
    slowness_slabs,
    slab_map,
    reference_gaps,
    reference_index,
    frequency_bins,
    shot_corner,
):
    slots_here = source_field.shape[1]
    rows_x = source_field.shape[2]
    cols_y = source_field.shape[3]
    tables = (
        transform_table(rows_x, True),
        transform_table(cols_y, True),
        transform_table(rows_x, False),
        transform_table(cols_y, False),
    )
    wave_x = wave_numbers(rows_x)
    wave_y = wave_numbers(cols_y)
    squares = wave_x[:, None] ** 2 + wave_y[None, :] ** 2
    freq_rank = lax.axis_index("freq")
    my_bins = lax.dynamic_slice_in_dim(frequency_bins, freq_rank * slots_here, slots_here)
    omegas = my_bins.astype(jnp.float32) * (2.0 * math.pi * bin_hertz)
    lag_weights = lag_table(frequency_bins, LAGS)
    direction = jnp.array([1.0, -1.0], jnp.float32)
    wave_stack = jnp.stack([source_field, receiver_field])
    slab_count = slowness_slabs.shape[0]
    corner_x = shot_corner[0]
    corner_y = shot_corner[1]
    crosses = []
    for depth_step in range(DEPTHS):
        global_slab = slab_map[depth_step]
        owner_rank = global_slab // slab_count
        local_pick = global_slab % slab_count
        own_window = lax.dynamic_slice(
            slowness_slabs, (local_pick, corner_x, corner_y), (1, rows_x, cols_y)
        )[0]
        window = spread(own_window, "freq", owner_rank)
        slowness = window.astype(jnp.float32)
        references = slow_base + jnp.cumsum(reference_gaps[depth_step])
        bracket = reference_index[depth_step]
        stepped = [
            extrapolate(
                wave_stack[:, :, 0],
                omegas[0],
                slowness,
                references,
                bracket,
                direction,
                tables,
                squares,
            )
        ]
        wave_stack = jnp.stack(stepped, axis=2)
        crosses.append(cross_product(wave_stack))
    all_crosses = jnp.stack(crosses)
    return lag_image_depths(
        lax.all_to_all(all_crosses, "freq", split_axis=3, concat_axis=2, tiled=True), lag_weights
    )


def solution(mesh):
    placed = (
        P("grp", "freq", None, None),
        P("grp", "freq", None, None),
        P(("grp", "freq"), None, None),
        P("grp"),
        P("grp", None),
        P("grp", None, None),
        P(),
        P("grp"),
    )
    return jax.shard_map(
        shards, mesh=mesh, in_specs=placed, out_specs=P("grp", "freq", None, None), check_vma=False
    )
```

profile of v0, /device:TPU:9, one launch (start us, length us, event | category | flops | bytes accessed | tf_op | source)
XLA Modules:
  0.0 221.5 jit_solution(4472801695292932038)
XLA Ops:
  6.5 1.3 fusion.162
  10.4 1.3 fusion.161
  14.3 2.0 select_bitcast_fusion
  16.3 4.4 %negate_convert_fusion = (bf16[1,512,512]{2,1,0:T(8,128)(2,1)S(1)}, bf16[1,512,512]{2,1,0:T(8,128)(2,1)S(1)}) fusion(), kind=kLoop, calls=%fused_computation.150 | loop fusion | flops 4980736 | bytes 1048576 | tf_op jit(solution)/shard_map/convert.25
  20.7 4.0 %fusion.115 = bf16[1,512,512]{2,1,0:T(8,128)(2,1)S(1)} fusion(), kind=kLoop, calls=%fused_computation.157 | loop fusion | flops 4194304 | bytes 524288 | tf_op jit(solution)/shard_map/convert.21
  24.7 1.1 negate_convert_fusion.1
  28.5 1.8 fusion.89
  30.3 1.0 fusion.128
  31.3 3.7 %convolution_bitcast_fusion.1 = f32[2,2,512,256]{2,3,1,0:T(8,128)S(1)} fusion(bf16[1,2,512,512]{3,2,0,1:T(8,128)(2,1)S(1)} %get-tuple-element.38, bf16[1,2,512,512]{3,2,0,1:T(8,128)(2,1)} %get-tuple-element.49, bf16[1,2,1,512,256]{4,3,1,0,2:T(8,128)(2,1)} %bitcast.250, bf16[1,2,1,512,256]{4,3,1,0,2:T(8,128)(2,1)} %bitcast.251, ...), kind=kOutput, calls=%fused_computation.63 | convolution fusion | flops 1618477056 | bytes 5767168 | tf_op jit(solution)/shard_map/cdxk,fcxy->fdky/dot_general | solution.py:74
  35.9 14.4 %fusion.59 = (f32[3,512,256]{1,2,0:T(8,128)}, f32[3,512,256]{1,2,0:T(8,128)}, f32[3,512,256]{1,2,0:T(8,128)S(1)}, f32[3,512,256]{1,2,0:T(8,128)S(1)}) fusion(f32[3]{0:T(128)S(1)} %get-tuple-element.73, f32[512,256]{0,1:T(8,128)S(1)} %broadcast_add_fusion, f32[3]{0:T(128)S(1)} %get-tuple-element.85), kind=kLoop, calls=%fused_computation.81 | loop fusion | flops 7077888 | bytes 6815768 | tf_op jit(solution)/shard_map/mul | solution.py:56
  50.4 1.1 fusion.1
  51.5 9.4 %fusion.27 = f32[2,3,2,512,256]{3,4,1,0,2:T(8,128)} fusion(bf16[2,3,1,512,256]{3,4,2,1,0:T(8,128)(2,1)S(1)} %get-tuple-element.18, bf16[2,3,1,512,256]{3,4,2,1,0:T(8,128)(2,1)S(1)} %get-tuple-element.17, bf16[1,2,512,512]{3,2,1,0:T(8,128)(2,1)} %get-tuple-element.50, bf16[1,2,512,512]{3,2,1,0:T(8,128)(2,1)} %get-tuple-element.37, ...), kind=kOutput, calls=%fused_computation.31 | convolution fusion | flops 4844158976 | bytes 12058624 | tf_op jit(solution)/shard_map/fjcxy,cdyk->fjdxk/dot_general | solution.py:85
  61.5 46.2 %all-reduce.3.cloned.1.call-done = (bf16[512,256]{1,0:T(8,128)(2,1)}, bf16[512,256]{1,0:T(8,128)(2,1)}) async-done(((bf16[512,256]{1,0:T(8,128)(2,1)}, bf16[512,256]{1,0:T(8,128)(2,1)}), (bf16[512,256]{1,0:T(8,128)(2,1)}, bf16[512,256]{1,0:T(8,128)(2,1)})) %all-reduce.3.cloned.1.call-update) | async-done | bytes 524304 | tf_op jit(solution)/shard_map/psum | solution.py:18
  107.8 6.4 %broadcast_subtract_fusion = (f32[512,256]{1,0:T(8,128)}, pred[512,256]{1,0:T(8,128)(4,1)S(1)}, f32[512,256]{1,0:T(8,128)S(1)}, pred[512,256]{1,0:T(8,128)(4,1)S(1)}) fusion(f32[]{:T(128)} %bitcast.64, f32[]{:T(128)} %bitcast.63, f32[]{:T(128)} %bitcast.62, bf16[512,256]{1,0:T(8,128)(2,1)} %get-tuple-element.6, s32[2,512,256]{2,1,0:T(8,128)} %param.14, ...), kind=kLoop, calls=%fused_computation.202 | loop fusion | flops 2359296 | bytes 2883608 | tf_op jit(solution)/shard_map/sub | solution.py:96
  114.4 2.2 select_subtract_fusion.5
  116.9 3.1 %fusion.121 = (f32[512,256]{1,0:T(8,128)}, f32[512,256]{1,0:T(8,128)}, f32[512,256]{1,0:T(8,128)}) fusion(pred[512,256]{1,0:T(8,128)(4,1)S(1)} %get-tuple-element.8, f32[]{:T(128)} %bitcast.64, f32[]{:T(128)} %bitcast.63, f32[]{:T(128)} %bitcast.62, bf16[512,256]{1,0:T(8,128)(2,1)S(1)} %copy-done.9), kind=kLoop, calls=%fused_computation.167 | loop fusion | flops 1048576 | bytes 1966092 | tf_op jit(solution)/shard_map/jit(clip)/min | solution.py:93
  120.0 1.1 copy.56
  121.0 1.0 copy.66
  124.0 3.7 %fusion.35 = (f32[2,2,512,256]{2,3,0,1:T(8,128)S(1)}, f32[2,2,512,256]{2,3,0,1:T(8,128)S(1)}) fusion(f32[2,3,2,512,256]{3,4,1,0,2:T(8,128)} %fusion.27, pred[512,256]{0,1:T(8,128)(4,1)S(1)} %copy.57), kind=kLoop, calls=%fused_computation.45 | loop fusion | flops 1048576 | bytes 10616832 | tf_op jit(solution)/shard_map/jit(_where)/select_n | solution.py:89
  127.8 9.0 %fusion.100 = (f32[2,1,512,256]{2,3,0,1:T(8,128)S(1)}, f32[2,1,512,256]{2,3,0,1:T(8,128)S(1)}, f32[2,1,512,256]{2,3,0,1:T(8,128)S(1)}, f32[2,1,512,256]{2,3,0,1:T(8,128)}) fusion(f32[2,2,512,256]{2,3,0,1:T(8,128)S(1)} %get-tuple-element.13, f32[512,256]{0,1:T(8,128)S(1)} %copy-done, f32[2]{0:T(128)S(1)} %multiply_multiply_fusion.4, ...), kind=kLoop, calls=%fused_computation.133 | loop fusion | flops 3670016 | bytes 9437192 | tf_op jit(solution)/shard_map/sub | solution.py:62
  136.8 5.6 %convolution_bitcast_fusion = f32[2,2,512,256]{2,3,1,0:T(8,128)} fusion(bf16[1,2,512,512]{3,2,0,1:T(8,128)(2,1)} %copy-done.14, bf16[1,2,512,512]{3,2,0,1:T(8,128)(2,1)} %get-tuple-element.49, bf16[1,2,256,256]{2,3,0,1:T(8,128)(2,1)} %get-tuple-element.58, bf16[1,2,256,256]{2,3,0,1:T(8,128)(2,1)} %get-tuple-element.61, ...), kind=kOutput, calls=%fused_computation.62 | convolution fusion | flops 1619525632 | bytes 9961472 | tf_op jit(solution)/shard_map/cdxk,fcxy->fdky/dot_general | solution.py:74
  142.4 2.1 fusion.106
  146.4 1.2 copy-done.7
  148.1 1.1 fusion.5
  149.6 3.6 %fusion.11 = bf16[2,3,2,512,256,1]{3,4,2,1,0,5:T(8,128)(2,1)S(1)} fusion(bf16[2,3,1,512,256]{3,4,2,1,0:T(8,128)(2,1)S(1)} %get-tuple-element.16, bf16[2,3,1,512,256]{3,4,2,1,0:T(8,128)(2,1)S(1)} %get-tuple-element.15, bf16[1,2,512,512]{3,2,1,0:T(8,128)(2,1)S(1)} %copy-done.13, bf16[1,2,512,512]{3,2,1,0:T(8,128)(2,1)S(1)} %copy-done.12), kind=kOutput, calls=%fused_computation.17 | convolution fusion | flops 3233284096 | bytes 8388608 | tf_op jit(solution)/shard_map/cdxk,fjcxy->fjdky/dot_general | solution.py:82
  153.2 4.5 %fusion.24 = f32[2,3,2,512,256]{3,4,0,2,1:T(8,128)} fusion(bf16[2,3,2,512,256,1]{3,4,2,1,0,5:T(8,128)(2,1)S(1)} %fusion.11, bf16[1,2,256,256]{2,3,1,0:T(8,128)(2,1)S(1)} %copy-done.11, bf16[1,2,256,256]{2,3,1,0:T(8,128)(2,1)S(1)} %get-tuple-element.57), kind=kOutput, calls=%fused_computation.30 | convolution fusion | flops 1610874880 | bytes 9961472 | tf_op jit(solution)/shard_map/fjcxy,cdyk->fjdxk/dot_general | solution.py:85
  159.2 3.7 %fusion.33 = (f32[2,2,512,256]{2,3,0,1:T(8,128)S(1)}, f32[2,2,512,256]{2,3,0,1:T(8,128)S(1)}) fusion(f32[2,3,2,512,256]{3,4,0,2,1:T(8,128)} %fusion.24, pred[512,256]{0,1:T(8,128)(4,1)S(1)} %copy.69), kind=kLoop, calls=%fused_computation.40 | loop fusion | flops 1048576 | bytes 10616832 | tf_op jit(solution)/shard_map/jit(_where)/select_n | solution.py:89
  162.9 8.0 %fusion.95 = (f32[2,1,1,512,256]{3,4,0,2,1:T(8,128)S(1)}, f32[2,1,1,512,256]{3,4,0,2,1:T(8,128)S(1)}, f32[2,1,1,512,256]{3,4,0,2,1:T(8,128)S(1)}, f32[2,1,1,512,256]{3,4,0,2,1:T(8,128)S(1)}) fusion(f32[2,2,512,256]{2,3,0,1:T(8,128)S(1)} %get-tuple-element.11, f32[512,256]{0,1:T(8,128)S(1)} %copy.68, f32[2]{0:T(128)S(1)} %multiply_multiply_fusion.4, ...), kind=kLoop, calls=%fused_computation.128 | loop fusion | flops 3670016 | bytes 9437192 | tf_op jit(solution)/shard_map/stack | solution.py:60
  172.6 2.1 copy.79
  174.7 6.5 %all-to-all-start = ((bf16[2,2,1,512,256]{4,0,2,1,3:T(2,128)(2,1)}), bf16[2,2,1,512,256]{4,0,2,1,3:T(2,128)(2,1)S(1)}, u32[]{:S(2)}, u32[]{:S(2)}) async-start(bf16[2,2,1,512,256]{4,0,2,1,3:T(2,128)(2,1)} %copy.79), calls=%async_computation | async-start | bytes 2097152 | tf_op jit(solution)/shard_map/all_to_all | solution.py:174
  181.3 24.8 %all-to-all-done = bf16[2,2,1,512,256]{4,0,2,1,3:T(2,128)(2,1)S(1)} async-done(((bf16[2,2,1,512,256]{4,0,2,1,3:T(2,128)(2,1)}), bf16[2,2,1,512,256]{4,0,2,1,3:T(2,128)(2,1)S(1)}, u32[]{:S(2)}, u32[]{:S(2)}) %all-to-all-start) | async-done | bytes 1048608 | tf_op jit(solution)/shard_map/all_to_all | solution.py:174
  206.1 8.6 %bitcast_multiply_fusion = f32[2,32,256,256]{3,2,1,0:T(8,128)} fusion(bf16[2,2,16,32,256]{4,0,1,3,2:T(2,128)(2,1)S(1)} %bitcast.249, bf16[1,16,256]{2,1,0:T(8,128)(2,1)S(1)} %get-tuple-element.64, bf16[1,16,256]{2,1,0:T(8,128)(2,1)S(1)} %get-tuple-element.63), kind=kOutput, calls=%fused_computation | convolution fusion | flops 272637952 | bytes 17842176 | tf_op jit(solution)/shard_map/dcwab,cwl->dabl/dot_general | solution.py:102
  (67 shorter events, 12.0 us)
Async XLA Ops:
  6.5 20.3 %copy-start.18 = (s32[16]{0:T(128)S(1)}, s32[16]{0:T(128)}, u32[]{:S(2)}) copy-start(s32[16]{0:T(128)} %param.15) | copy-start | bytes 196
  6.5 21.6 %copy-start.17 = (f32[2,3]{1,0:T(2,128)S(1)}, f32[2,3]{1,0:T(2,128)}, u32[]{:S(2)}) copy-start(f32[2,3]{1,0:T(2,128)} %param.13) | copy-start | bytes 76
  6.5 101.2 %all-reduce.3.cloned.1.call-start = ((), (), s32[]{:S(2)}) async-start(), calls=%async_computation.1 | async-start | bytes 1048576 | tf_op jit(solution)/shard_map/psum | solution.py:18
  30.3 4.7 %copy-start.14 = (bf16[1,2,512,512]{3,2,0,1:T(8,128)(2,1)}, bf16[1,2,512,512]{3,2,0,1:T(8,128)(2,1)S(1)}, u32[]{:S(2)}) copy-start(bf16[1,2,512,512]{3,2,0,1:T(8,128)(2,1)S(1)} %get-tuple-element.38) | copy-start | bytes 3145732
  35.9 14.4 %copy-start.16 = (f32[2]{0:T(128)S(1)}, f32[2]{0:T(128)}, u32[]{:S(2)}) copy-start(f32[2]{0:T(128)} %constant.135.clone) | copy-start | bytes 28
  107.8 6.7 %copy-start.10 = (bf16[512,256]{1,0:T(8,128)(2,1)S(1)}, bf16[512,256]{1,0:T(8,128)(2,1)}, u32[]{:S(2)}) copy-start(bf16[512,256]{1,0:T(8,128)(2,1)} %get-tuple-element.5) | copy-start | bytes 786436
  107.8 9.1 %copy-start.9 = (bf16[512,256]{1,0:T(8,128)(2,1)S(1)}, bf16[512,256]{1,0:T(8,128)(2,1)}, u32[]{:S(2)}) copy-start(bf16[512,256]{1,0:T(8,128)(2,1)} %get-tuple-element.6) | copy-start | bytes 786436
  124.0 3.7 %copy-start = (f32[512,256]{0,1:T(8,128)S(1)}, f32[512,256]{0,1:T(8,128)}, u32[]{:S(2)}) copy-start(f32[512,256]{0,1:T(8,128)} %copy.56) | copy-start | bytes 1572868
  124.0 3.8 %copy-start.1 = (f32[512,256]{0,1:T(8,128)S(1)}, f32[512,256]{0,1:T(8,128)}, u32[]{:S(2)}) copy-start(f32[512,256]{0,1:T(8,128)} %copy.66) | copy-start | bytes 1572868
  144.5 1.7 copy-start.2
  146.2 1.4 copy-start.7
  146.2 1.9 copy-start.8
  148.1 1.2 copy-start.12
  148.1 1.5 copy-start.13
  149.6 3.6 %copy-start.11 = (bf16[1,2,256,256]{2,3,1,0:T(8,128)(2,1)S(1)}, bf16[1,2,256,256]{2,3,1,0:T(8,128)(2,1)}, u32[]{:S(2)}) copy-start(bf16[1,2,256,256]{2,3,1,0:T(8,128)(2,1)} %get-tuple-element.62) | copy-start | bytes 786436
  153.2 4.5 %copy-start.6 = (f32[512,256]{1,0:T(8,128)S(1)}, f32[512,256]{1,0:T(8,128)}, u32[]{:S(2)}) copy-start(f32[512,256]{1,0:T(8,128)} %get-tuple-element.53) | copy-start | bytes 1572868
  153.2 4.7 %copy-start.5 = (f32[512,256]{1,0:T(8,128)S(1)}, f32[512,256]{1,0:T(8,128)}, u32[]{:S(2)}) copy-start(f32[512,256]{1,0:T(8,128)} %get-tuple-element.52) | copy-start | bytes 1572868
  157.8 1.0 copy-start.4
  157.8 1.2 copy-start.3
  171.5 1.0 copy-start.15
  174.7 31.4 %all-to-all-start = ((bf16[2,2,1,512,256]{4,0,2,1,3:T(2,128)(2,1)}), bf16[2,2,1,512,256]{4,0,2,1,3:T(2,128)(2,1)S(1)}, u32[]{:S(2)}, u32[]{:S(2)}) async-start(bf16[2,2,1,512,256]{4,0,2,1,3:T(2,128)(2,1)} %copy.79), calls=%async_computation | async-start | bytes 2097152 | tf_op jit(solution)/shard_map/all_to_all | solution.py:174
Sparse Core Ops, SparseCore 0:
  16.4 91.2 all-reduce.2
where the time goes:
time: 222 us; the launch traced here: 221 us
  other arithmetic  72.8 us (33%)
  waiting for transfers between devices  71 us (32%)
  matrix products  35.3 us (16%)
  between operations  19.5 us (9%)
  local copies, waits for them, and re-layouts  16.4 us (7%)
  starting transfers between devices  6.48 us (3%)
    psum x1, waiting for transfers between devices, spread(): return lax.psum(block, axis)  46.2 us
    all_to_all x1, waiting for transfers between devices, shards(): lax.all_to_all(all_crosses, 'freq', split_axis=3, concat_axis=2, tiled=True)  24.8 us
    another operation x11, other arithmetic  14.5 us
    mul x1, other arithmetic, phase_factors(): fading * jnp.cos(vertical * layer_thick)  14.4 us
    dot_general x2, matrix products, extrapolate(): jnp.einsum('fjcxy,cdyk->fjdxk', returned, inverse_y, preferred_element_ty...  13.9 us
    dot_general x2, matrix products, extrapolate(): jnp.einsum('cdxk,fcxy->fdky', forward_x, half_done, preferred_element_typ...  9.22 us
    sub x1, other arithmetic, rotate(): jnp.cos(turn_angle) * field_pair[:, 0]  9.01 us
    dot_general x1, matrix products, lag_image_depths(): jnp.einsum('dcwab,cwl->dabl', cross_spec, lag_weights, preferred_element_...  8.56 us
  transfers between devices with their start and end apart: 2, of which 2 were waited for; matrix products, arithmetic and copies ran while one was open for 20% of the time, Pallas kernels for 0%

commit v1 on v0

--- a/solution.py
+++ b/solution.py
@@ -15,7 +15,7 @@
 
 def spread(block, axis, holder):
     block = jnp.where(lax.axis_index(axis) == holder, block, jnp.zeros_like(block))
-    return lax.psum(block, axis)
+    return jnp.sum(lax.all_gather(block, axis), axis=0)
 
 
 def transform_table(length, forward):

time: 222 us -> 237 us (1.068)
  other arithmetic: 72.8 us -> 82.6 us
  waiting for transfers between devices: 71 us -> 77.1 us
  starting transfers between devices: 6.48 us -> 3.88 us
    all_gather x0 -> x2, waiting for transfers between devices: none -> 51.7 us  [spread(): return jnp.sum(lax.all_gather(block, axis), axis=0)]
    psum x1 -> x0, waiting for transfers between devices: 46.2 us -> none  [spread(): return lax.psum(block, axis)]
    reduce_sum x0 -> x2, other arithmetic: none -> 5.7 us  [spread(): return jnp.sum(lax.all_gather(block, axis), axis=0)]
    mul x1 -> x3, other arithmetic: 0.01 us -> 4.97 us  [extrapolate(): direction[:, None, None] * angular * layer_thick]
    all_to_all x1, starting transfers between devices: 6.48 us -> 3.83 us  [shards(): lax.all_to_all(all_crosses, 'freq', split_axis=3, concat_axis=2, tiled=True)]
    sub x4 -> x0, local copies, waits for them, and re-layouts: 2.47 us -> none  [the longest x2 1.25 us: extrapolate(): weight = jnp.clip((slowness - slow_low) / (slow_high - slow_low), 0.0, 1.0)]
    mul x0 -> x4, local copies, waits for them, and re-layouts: none -> 2.4 us  [extrapolate(): direction[:, None, None] * angular * layer_thick]
    min x1 -> x2, other arithmetic: 3.13 us -> 4.89 us  [extrapolate(): weight = jnp.clip((slowness - slow_low) / (slow_high - slow_low), 0.0, 1.0)]
  transfers between devices with their start and end apart: 2 -> 3, of which waited for: 2 -> 3; matrix products, arithmetic and copies ran while one was open for 20% -> 21% of each run, Pallas kernels for 0% -> 0%
where the time goes in v1:
time: 237 us
  other arithmetic  82.6 us (35%)
  waiting for transfers between devices  77.1 us (33%)
  matrix products  35.1 us (15%)
  between operations  19.3 us (8%)
  local copies, waits for them, and re-layouts  18.5 us (8%)
  starting transfers between devices  3.88 us (2%)
    all_gather x2, waiting for transfers between devices, spread(): return jnp.sum(lax.all_gather(block, axis), axis=0)  51.7 us
    all_to_all x1, waiting for transfers between devices, shards(): lax.all_to_all(all_crosses, 'freq', split_axis=3, concat_axis=2, tiled=True)  24.8 us
    another operation x11, other arithmetic  14.6 us
    mul x1, other arithmetic, phase_factors(): fading * jnp.cos(vertical * layer_thick)  14.4 us
    dot_general x2, matrix products, extrapolate(): jnp.einsum('fjcxy,cdyk->fjdxk', returned, inverse_y, preferred_element_ty...  13.9 us
    dot_general x2, matrix products, extrapolate(): jnp.einsum('cdxk,fcxy->fdky', forward_x, half_done, preferred_element_typ...  9.09 us
    sub x1, other arithmetic, rotate(): jnp.cos(turn_angle) * field_pair[:, 0]  9.01 us
    dot_general x1, matrix products, lag_image_depths(): jnp.einsum('dcwab,cwl->dabl', cross_spec, lag_weights, preferred_element_...  8.56 us
  transfers between devices with their start and end apart: 3, of which 3 were waited for; matrix products, arithmetic and copies ran while one was open for 21% of the time, Pallas kernels for 0%

profile of v1, /device:TPU:9, one launch (start us, length us, event | category | flops | bytes accessed | tf_op | source)
XLA Modules:
  0.0 236.5 jit_solution(13554519867425050647)
XLA Ops:
  6.5 1.3 fusion.166
  10.3 1.3 fusion.164
  14.1 2.0 broadcast_select_fusion
  16.9 1.2 dynamic_slice.10
  23.3 4.0 %fusion.115 = bf16[1,512,512]{2,1,0:T(8,128)(2,1)S(1)} fusion(), kind=kLoop, calls=%fused_computation.157 | loop fusion | flops 4194304 | bytes 524288 | tf_op jit(solution)/shard_map/convert.25
  27.3 4.4 %negate_convert_fusion = (bf16[1,512,512]{2,1,0:T(8,128)(2,1)S(1)}, bf16[1,512,512]{2,1,0:T(8,128)(2,1)S(1)}) fusion(), kind=kLoop, calls=%fused_computation.150 | loop fusion | flops 4980736 | bytes 1048576 | tf_op jit(solution)/shard_map/convert.29
  32.7 1.8 fusion.89
  35.5 3.5 %convolution_bitcast_fusion.1 = f32[2,2,512,256]{2,3,1,0:T(8,128)S(1)} fusion(bf16[1,2,512,512]{3,2,0,1:T(8,128)(2,1)S(1)} %get-tuple-element.36, bf16[1,2,512,512]{3,2,0,1:T(8,128)(2,1)} %get-tuple-element.47, bf16[1,2,1,512,256]{4,3,1,0,2:T(8,128)(2,1)} %bitcast.278, bf16[1,2,1,512,256]{4,3,1,0,2:T(8,128)(2,1)} %bitcast.279, ...), kind=kOutput, calls=%fused_computation.63 | convolution fusion | flops 1618477056 | bytes 5767168 | tf_op jit(solution)/shard_map/cdxk,fcxy->fdky/dot_general | solution.py:74
  40.1 14.4 %fusion.59 = (f32[3,512,256]{1,2,0:T(8,128)}, f32[3,512,256]{1,2,0:T(8,128)}, f32[3,512,256]{1,2,0:T(8,128)S(1)}, f32[3,512,256]{1,2,0:T(8,128)S(1)}) fusion(f32[3]{0:T(128)S(1)} %get-tuple-element.71, f32[512,256]{0,1:T(8,128)S(1)} %copy-done.16, f32[3]{0:T(128)S(1)} %get-tuple-element.81), kind=kLoop, calls=%fused_computation.81 | loop fusion | flops 7077888 | bytes 6815768 | tf_op jit(solution)/shard_map/mul | solution.py:56
  55.7 9.4 %fusion.27 = f32[2,3,2,512,256]{3,4,1,0,2:T(8,128)} fusion(bf16[2,3,1,512,256]{3,4,2,1,0:T(8,128)(2,1)S(1)} %get-tuple-element.16, bf16[2,3,1,512,256]{3,4,2,1,0:T(8,128)(2,1)S(1)} %get-tuple-element.15, bf16[1,2,512,512]{3,2,1,0:T(8,128)(2,1)} %get-tuple-element.48, bf16[1,2,512,512]{3,2,1,0:T(8,128)(2,1)} %get-tuple-element.35, ...), kind=kOutput, calls=%fused_computation.31 | convolution fusion | flops 4844158976 | bytes 12058624 | tf_op jit(solution)/shard_map/fjcxy,cdyk->fjdxk/dot_general | solution.py:85
  65.1 3.4 %all-gather.3.cloned.1.call-done = bf16[16,512,256]{2,1,0:T(8,128)(2,1)} async-done(((bf16[1,512,256]{2,1,0:T(8,128)(2,1)}), bf16[16,512,256]{2,1,0:T(8,128)(2,1)}) %all-gather.3.cloned.1.call-update) | async-done | bytes 4194320 | tf_op jit(solution)/shard_map/all_gather | solution.py:18
  68.4 2.9 %reduce_sum.24 = bf16[512,256]{1,0:T(8,128)(2,1)S(1)} reduce(bf16[16,512,256]{2,1,0:T(8,128)(2,1)} %all-gather.3.cloned.1.call-done, bf16[]{:T(256)} %constant.116.clone.1), dimensions={0}, to_apply=%region_0.1 | reduce | flops 1966080 | bytes 4456450 | tf_op jit(solution)/shard_map/reduce_sum | solution.py:18
  71.3 48.3 %all-gather.5.cloned.1.call-done = bf16[16,512,256]{2,1,0:T(8,128)(2,1)} async-done(((bf16[1,512,256]{2,1,0:T(8,128)(2,1)}), bf16[16,512,256]{2,1,0:T(8,128)(2,1)}) %all-gather.5.cloned.1.call-update) | async-done | bytes 4194320 | tf_op jit(solution)/shard_map/all_gather | solution.py:18
  119.6 2.9 %reduce_sum.25 = bf16[512,256]{1,0:T(8,128)(2,1)S(1)} reduce(bf16[16,512,256]{2,1,0:T(8,128)(2,1)} %all-gather.5.cloned.1.call-done, bf16[]{:T(256)} %constant.116.clone.1), dimensions={0}, to_apply=%region_2.3 | reduce | flops 1966080 | bytes 4456450 | tf_op jit(solution)/shard_map/reduce_sum | solution.py:18
  122.4 5.0 %broadcast_subtract_fusion = (f32[512,256]{1,0:T(8,128)}, pred[1,512,256]{2,1,0:T(8,128)(4,1)S(1)}, f32[512,256]{1,0:T(8,128)S(1)}, pred[1,512,256]{2,1,0:T(8,128)(4,1)S(1)}) fusion(f32[]{:T(128)} %bitcast.65, f32[]{:T(128)} %bitcast.64, f32[]{:T(128)} %bitcast.63, bf16[512,256]{1,0:T(8,128)(2,1)S(1)} %reduce_sum.25, s32[2,512,256]{2,1,0:T(8,128)S(1)} %copy-done.9, ...), kind=kLoop, calls=%fused_computation.206 | loop fusion | flops 2359296 | bytes 2883608 | tf_op jit(solution)/shard_map/sub | solution.py:96
  127.4 2.1 fusion.124
  129.5 2.1 fusion.127
  131.6 2.9 %fusion.122 = (f32[512,256]{1,0:T(8,128)}, f32[512,256]{1,0:T(8,128)}) fusion(bf16[512,256]{1,0:T(8,128)(2,1)S(1)} %reduce_sum.25, pred[1,512,256]{2,1,0:T(8,128)(4,1)S(1)} %get-tuple-element.6, f32[]{:T(128)} %bitcast.64, f32[]{:T(128)} %bitcast.63, f32[]{:T(128)} %bitcast.65), kind=kLoop, calls=%fused_computation.168 | loop fusion | flops 655360 | bytes 1441804 | tf_op jit(solution)/shard_map/mul | solution.py:94
  134.5 2.8 %fusion.129 = f32[512,256]{1,0:T(8,128)} fusion(bf16[512,256]{1,0:T(8,128)(2,1)S(1)} %reduce_sum.25, f32[]{:T(128)} %bitcast.65, f32[]{:T(128)} %bitcast.64, f32[]{:T(128)} %bitcast.63, pred[1,512,256]{2,1,0:T(8,128)(4,1)S(1)} %get-tuple-element.6), kind=kLoop, calls=%fused_computation.175 | loop fusion | flops 917504 | bytes 917516 | tf_op jit(solution)/shard_map/jit(clip)/min | solution.py:93
  141.5 3.7 %fusion.35 = (f32[2,2,512,256]{2,3,0,1:T(8,128)S(1)}, f32[2,2,512,256]{2,3,0,1:T(8,128)S(1)}) fusion(f32[2,3,2,512,256]{3,4,1,0,2:T(8,128)} %fusion.27, pred[512,256]{0,1:T(8,128)(4,1)S(1)} %copy.57), kind=kLoop, calls=%fused_computation.45 | loop fusion | flops 1048576 | bytes 10616832 | tf_op jit(solution)/shard_map/jit(_where)/select_n | solution.py:89
  145.3 9.0 %fusion.100 = (f32[2,1,512,256]{2,3,0,1:T(8,128)S(1)}, f32[2,1,512,256]{2,3,0,1:T(8,128)S(1)}, f32[2,1,512,256]{2,3,0,1:T(8,128)S(1)}, f32[2,1,512,256]{2,3,0,1:T(8,128)}) fusion(f32[2,2,512,256]{2,3,0,1:T(8,128)S(1)} %get-tuple-element.11, f32[512,256]{0,1:T(8,128)S(1)} %copy-done.2, f32[2]{0:T(128)S(1)} %multiply_multiply_fusion.4, ...), kind=kLoop, calls=%fused_computation.133 | loop fusion | flops 3670016 | bytes 9437192 | tf_op jit(solution)/shard_map/sub | solution.py:62
  154.3 5.6 %convolution_bitcast_fusion = f32[2,2,512,256]{2,3,1,0:T(8,128)} fusion(bf16[1,2,512,512]{3,2,0,1:T(8,128)(2,1)} %copy-done.13, bf16[1,2,512,512]{3,2,0,1:T(8,128)(2,1)} %get-tuple-element.47, bf16[1,2,256,256]{2,3,0,1:T(8,128)(2,1)} %get-tuple-element.54, bf16[1,2,256,256]{2,3,0,1:T(8,128)(2,1)} %get-tuple-element.57, ...), kind=kOutput, calls=%fused_computation.62 | convolution fusion | flops 1619525632 | bytes 9961472 | tf_op jit(solution)/shard_map/cdxk,fcxy->fdky/dot_general | solution.py:74
  159.9 2.1 fusion.106
  164.0 1.2 copy-done.7
  167.2 3.6 %fusion.11 = bf16[2,3,2,512,256,1]{3,4,2,1,0,5:T(8,128)(2,1)S(1)} fusion(bf16[2,3,1,512,256]{3,4,2,1,0:T(8,128)(2,1)S(1)} %get-tuple-element.14, bf16[2,3,1,512,256]{3,4,2,1,0:T(8,128)(2,1)S(1)} %get-tuple-element.13, bf16[1,2,512,512]{3,2,1,0:T(8,128)(2,1)S(1)} %copy-done.12, bf16[1,2,512,512]{3,2,1,0:T(8,128)(2,1)S(1)} %copy-done.11), kind=kOutput, calls=%fused_computation.17 | convolution fusion | flops 3233284096 | bytes 8388608 | tf_op jit(solution)/shard_map/cdxk,fjcxy->fjdky/dot_general | solution.py:82
  170.8 4.5 %fusion.24 = f32[2,3,2,512,256]{3,4,0,2,1:T(8,128)} fusion(bf16[2,3,2,512,256,1]{3,4,2,1,0,5:T(8,128)(2,1)S(1)} %fusion.11, bf16[1,2,256,256]{2,3,1,0:T(8,128)(2,1)S(1)} %copy-done.10, bf16[1,2,256,256]{2,3,1,0:T(8,128)(2,1)S(1)} %get-tuple-element.53), kind=kOutput, calls=%fused_computation.30 | convolution fusion | flops 1610874880 | bytes 9961472 | tf_op jit(solution)/shard_map/fjcxy,cdyk->fjdxk/dot_general | solution.py:85
  176.8 3.7 %fusion.33 = (f32[2,2,512,256]{2,3,0,1:T(8,128)S(1)}, f32[2,2,512,256]{2,3,0,1:T(8,128)S(1)}) fusion(f32[2,3,2,512,256]{3,4,0,2,1:T(8,128)} %fusion.24, pred[512,256]{0,1:T(8,128)(4,1)S(1)} %copy.69), kind=kLoop, calls=%fused_computation.40 | loop fusion | flops 1048576 | bytes 10616832 | tf_op jit(solution)/shard_map/jit(_where)/select_n | solution.py:89
  180.5 8.0 %fusion.95 = (f32[2,1,1,512,256]{3,4,0,2,1:T(8,128)S(1)}, f32[2,1,1,512,256]{3,4,0,2,1:T(8,128)S(1)}, f32[2,1,1,512,256]{3,4,0,2,1:T(8,128)S(1)}, f32[2,1,1,512,256]{3,4,0,2,1:T(8,128)S(1)}) fusion(f32[2,2,512,256]{2,3,0,1:T(8,128)S(1)} %get-tuple-element.9, f32[512,256]{0,1:T(8,128)S(1)} %copy.68, f32[2]{0:T(128)S(1)} %multiply_multiply_fusion.4, ...), kind=kLoop, calls=%fused_computation.128 | loop fusion | flops 3670016 | bytes 9437192 | tf_op jit(solution)/shard_map/stack | solution.py:60
  190.3 2.1 copy.79
  192.4 3.8 %all-to-all-start = ((bf16[2,2,1,512,256]{4,0,2,1,3:T(2,128)(2,1)}), bf16[2,2,1,512,256]{4,0,2,1,3:T(2,128)(2,1)S(1)}, u32[]{:S(2)}, u32[]{:S(2)}) async-start(bf16[2,2,1,512,256]{4,0,2,1,3:T(2,128)(2,1)} %copy.79), calls=%async_computation | async-start | bytes 2097152 | tf_op jit(solution)/shard_map/all_to_all | solution.py:174
  196.4 24.8 %all-to-all-done = bf16[2,2,1,512,256]{4,0,2,1,3:T(2,128)(2,1)S(1)} async-done(((bf16[2,2,1,512,256]{4,0,2,1,3:T(2,128)(2,1)}), bf16[2,2,1,512,256]{4,0,2,1,3:T(2,128)(2,1)S(1)}, u32[]{:S(2)}, u32[]{:S(2)}) %all-to-all-start) | async-done | bytes 1048608 | tf_op jit(solution)/shard_map/all_to_all | solution.py:174
  221.1 8.6 %bitcast_multiply_fusion = f32[2,32,256,256]{3,2,1,0:T(8,128)} fusion(bf16[2,2,16,32,256]{4,0,1,3,2:T(2,128)(2,1)S(1)} %bitcast.275, bf16[1,16,256]{2,1,0:T(8,128)(2,1)S(1)} %get-tuple-element.60, bf16[1,16,256]{2,1,0:T(8,128)(2,1)S(1)} %get-tuple-element.59), kind=kOutput, calls=%fused_computation | convolution fusion | flops 272637952 | bytes 17842176 | tf_op jit(solution)/shard_map/dcwab,cwl->dabl/dot_general | solution.py:102
  (74 shorter events, 21.0 us)
Async XLA Ops:
  6.5 61.9 %all-gather.3.cloned.1.call-start = ((), (), s32[]{:S(2)}) async-start(), calls=%async_computation.1 | async-start | bytes 4456448 | tf_op jit(solution)/shard_map/all_gather | solution.py:18
  16.1 103.4 %all-gather.5.cloned.1.call-start = ((), (), s32[]{:S(2)}) async-start(), calls=%async_computation.2 | async-start | bytes 4456448 | tf_op jit(solution)/shard_map/all_gather | solution.py:18
  32.7 1.8 copy-start.17
  34.5 4.6 %copy-start.13 = (bf16[1,2,512,512]{3,2,0,1:T(8,128)(2,1)}, bf16[1,2,512,512]{3,2,0,1:T(8,128)(2,1)S(1)}, u32[]{:S(2)}) copy-start(bf16[1,2,512,512]{3,2,0,1:T(8,128)(2,1)S(1)} %get-tuple-element.36) | copy-start | bytes 3145732
  39.1 1.0 copy-start.16
  71.3 51.1 %copy-start.9 = (s32[2,512,256]{2,1,0:T(8,128)S(1)}, s32[2,512,256]{2,1,0:T(8,128)}, u32[]{:S(2)}) copy-start(s32[2,512,256]{2,1,0:T(8,128)} %param.14) | copy-start | bytes 3145732
  141.5 3.7 %copy-start.2 = (f32[512,256]{0,1:T(8,128)S(1)}, f32[512,256]{0,1:T(8,128)}, u32[]{:S(2)}) copy-start(f32[512,256]{0,1:T(8,128)} %copy.56) | copy-start | bytes 1572868
  141.5 3.8 %copy-start.3 = (f32[512,256]{0,1:T(8,128)S(1)}, f32[512,256]{0,1:T(8,128)}, u32[]{:S(2)}) copy-start(f32[512,256]{0,1:T(8,128)} %copy.66) | copy-start | bytes 1572868
  162.0 1.8 copy-start.4
  163.8 1.4 copy-start.7
  163.8 1.9 copy-start.8
  165.7 1.2 copy-start.11
  165.7 1.5 copy-start.12
  167.2 3.6 %copy-start.10 = (bf16[1,2,256,256]{2,3,1,0:T(8,128)(2,1)S(1)}, bf16[1,2,256,256]{2,3,1,0:T(8,128)(2,1)}, u32[]{:S(2)}) copy-start(bf16[1,2,256,256]{2,3,1,0:T(8,128)(2,1)} %get-tuple-element.58) | copy-start | bytes 786436
  170.8 4.8 %copy-start.1 = (f32[512,256]{1,0:T(8,128)S(1)}, f32[512,256]{1,0:T(8,128)}, u32[]{:S(2)}) copy-start(f32[512,256]{1,0:T(8,128)} %get-tuple-element.49) | copy-start | bytes 1572868
  170.8 5.0 %copy-start = (f32[512,256]{1,0:T(8,128)S(1)}, f32[512,256]{1,0:T(8,128)}, u32[]{:S(2)}) copy-start(f32[512,256]{1,0:T(8,128)} %get-tuple-element.50) | copy-start | bytes 1572868
  175.4 1.0 copy-start.5
  175.4 1.2 copy-start.6
  189.1 1.0 copy-start.14
  189.1 1.0 copy-start.15
  190.3 6.0 %copy-start.18 = (s32[16]{0:T(128)S(1)}, s32[16]{0:T(128)}, u32[]{:S(2)}) copy-start(s32[16]{0:T(128)} %param.15) | copy-start | bytes 196
  192.4 28.8 %all-to-all-start = ((bf16[2,2,1,512,256]{4,0,2,1,3:T(2,128)(2,1)}), bf16[2,2,1,512,256]{4,0,2,1,3:T(2,128)(2,1)S(1)}, u32[]{:S(2)}, u32[]{:S(2)}) async-start(bf16[2,2,1,512,256]{4,0,2,1,3:T(2,128)(2,1)} %copy.79), calls=%async_computation | async-start | bytes 2097152 | tf_op jit(solution)/shard_map/all_to_all | solution.py:174
Sparse Core Ops, SparseCore 0:
  16.3 52.1 all-gather.2
  70.6 48.9 all-gather.4
